TPU v7x, 32 devices: a whole 2x2x4 slice. The times are simulated.
32 devices in a mesh: grp: 4 (over z), tile: 8 (over y, x, core).
Axes of the slice: x: 2, y: 2, z: 4, core: 2. Of those that a mesh axis runs over, the one named last changes fastest.
Arguments:
- right_side: float32 [16, 32768], P(None, ('grp', 'tile')), may hold values from -6 to 6
- ridge: float32 [32768], P(('grp', 'tile')), may hold values from 1 to 4
- tiles: float32 [128, 1024, 1024], P(('grp', 'tile')), may hold values from -0.013671875 to 0.013671875
- tile_list: int32 [128, 2], P(('grp', 'tile')), may hold values from 0 to 31, as said below
Outputs:
- solution: float32 [16, 32768], P(None, ('grp', 'tile'))
- residual: float32 [16, 32768], P(None, ('grp', 'tile'))
Inputs may be any that keep to these rules, and one draw needn't show every extreme that they name: `tile_list`: each row is a pair (row block, column block) with row block >= column block; no pair appears twice; rows stand in packed row-major order (row block rising, then column block rising).
All inputs are finite; a program needn't handle non-finite values.
Results may differ from a plain program's by a relative error of at most 0.0003.
Values sent between devices are 32-bit elements; how exact they have to be, the bound alone decides.
A program may use at most 64 MiB of HBM per device.

v0:
```python
import jax
import jax.numpy as jnp
from jax import lax
from jax.sharding import PartitionSpec as P

ITERS = 2


def gauss_solve(matrix, rhs):
    order = matrix.shape[0]
    for pivot in range(order):
        scale = 1.0 / matrix[pivot, pivot]
        row_new = matrix[pivot] * scale
        rhs_new = rhs[pivot] * scale
        factor = matrix[:, pivot] * (1.0 - (jnp.arange(order) == pivot).astype(matrix.dtype))
        matrix = matrix - factor[:, None] * row_new[None, :]
        rhs = rhs - factor[:, None] * rhs_new[None, :]
        matrix = matrix.at[pivot].set(row_new)
        rhs = rhs.at[pivot].set(rhs_new)
    return rhs


def gram(left, right):
    return lax.dot_general(
        left,
        right,
        (((1,), (1,)), ((), ())),
        precision=lax.Precision.HIGHEST,
        preferred_element_type=jnp.float32,
    )


def mixed(coeffs, rows):
    return jnp.dot(coeffs.T, rows, precision=lax.Precision.HIGHEST)


def tile_masks(order):
    rowid = lax.broadcasted_iota(jnp.int32, (order, order), 0)
    colid = lax.broadcasted_iota(jnp.int32, (order, order), 1)
    return (rowid >= colid, rowid > colid)


def apply_kernel(tiles, tile_list, field):
    order = tiles.shape[1]
    lower, strict = tile_masks(order)

    def step(total, item):
        tile, pair = item
        block_row = pair[0]
        block_col = pair[1]
        differ = block_row != block_col
        direct_tile = jnp.where(jnp.logical_or(lower, differ), tile, jnp.zeros_like(tile))
        mirror_tile = jnp.where(jnp.logical_or(strict, differ), tile, jnp.zeros_like(tile))
        row_start = block_row * order
        col_start = block_col * order
        from_col = lax.dynamic_slice_in_dim(field, col_start, order, 1)
        from_row = lax.dynamic_slice_in_dim(field, row_start, order, 1)
        into_row = lax.dot_general(
            from_col,
            direct_tile,
            (((1,), (1,)), ((), ())),
            precision=lax.Precision.HIGHEST,
            preferred_element_type=jnp.float32,
        )
        into_col = jnp.dot(
            from_row,
            mirror_tile,
            precision=lax.Precision.HIGHEST,
            preferred_element_type=jnp.float32,
        )
        total = lax.dynamic_update_slice_in_dim(
            total, lax.dynamic_slice_in_dim(total, row_start, order, 1) + into_row, row_start, 1
        )
        total = lax.dynamic_update_slice_in_dim(
            total, lax.dynamic_slice_in_dim(total, col_start, order, 1) + into_col, col_start, 1
        )
        return (total, None)

    start = jnp.zeros(field.shape, jnp.float32)
    total, _ = lax.scan(step, start, (tiles, tile_list))
    return total


def local(right_side, ridge, tiles, tile_list):
    local_width = right_side.shape[1]
    whole_rhs, whole_ridge = (
        lax.all_gather(right_side, ("grp", "tile"), axis=1, tiled=True),
        lax.all_gather(ridge, ("grp", "tile"), axis=0, tiled=True),
    )
    solution = jnp.zeros_like(whole_rhs)
    residual = whole_rhs
    direction = whole_rhs
    norm_now = gram(residual, residual)
    for step in range(ITERS):
        partial_image = apply_kernel(tiles, tile_list, direction)
        image = lax.psum(partial_image, ("grp", "tile")) + whole_ridge[None, :] * direction
        alpha = gauss_solve(gram(direction, image), norm_now)
        solution = solution + mixed(alpha, direction)
        residual = residual - mixed(alpha, image)
        if step + 1 < ITERS:
            norm_next = gram(residual, residual)
            beta = gauss_solve(norm_now, norm_next)
            direction = residual + mixed(beta, direction)
            norm_now = norm_next
    offset = lax.axis_index(("grp", "tile")) * local_width
    solution = lax.dynamic_slice_in_dim(solution, offset, local_width, 1)
    residual = lax.dynamic_slice_in_dim(residual, offset, local_width, 1)
    return (solution, residual)


def solution(mesh):
    return jax.shard_map(
        local,
        mesh=mesh,
        in_specs=(
            P(None, ("grp", "tile")),
            P(("grp", "tile")),
            P(("grp", "tile"), None, None),
            P(("grp", "tile"), None),
        ),
        out_specs=(P(None, ("grp", "tile")), P(None, ("grp", "tile"))),
        check_vma=False,
    )
```

profile of v0, /device:TPU:0, one launch (start us, length us, event | category | flops | bytes accessed | tf_op | source)
XLA Modules:
  0.0 568.2 jit_solution(14640766748409336953)
XLA Ops:
  8.0 62.1 %all-gather.2.cloned.1.call-done = f32[16,32768]{1,0:T(8,128)} async-done(((f32[16,1024]{1,0:T(8,128)}), f32[16,32768]{1,0:T(8,128)}) %all-gather.2.cloned.1.call-update) | async-done | bytes 2097168 | tf_op jit(solution)/shard_map/all_gather | solution.py:87
  72.4 57.3 %while.115 = (s32[]{:T(128)}, f32[16,32768]{1,0:T(8,128)}, s32[4,2]{0,1:T(2,128)S(1)}, f32[16,32768]{1,0:T(8,128)S(1)}, f32[4,1024,1024]{2,1,0:T(8,128)}, /*inde...) while((s32[]{:T(128)}, f32[16,32768]{1,0:T(8,128)}, s32[4,2]{0,1:T(2,128)S(1)}, ...), condition=%wide.region_1.2_spmd.clone, body=%wide.region_0.1_spmd.clone.sunk | while | flops 408977408 | bytes 8783110 | solution.py:80
  75.4 6.2 %fusion.231 = f32[16,32768]{1,0:T(8,128)} fusion(f32[16,32768]{1,0:T(8,128)} %get-tuple-element.1416, s32[]{:T(128)S(6)} %select_n.80, f32[4,1024,1024]{2,1,0:T(8,128)} %get-tuple-element.1428, s32[]{:T(128)S(6)} %copy.29, pred[]{:T(512)} %bitcast.292, f32[16,32768]{1,0:T(8,128)S(1)} %get-tuple-element.1427, s32[]{:T(128)S(6)} %select_n.81), kind=kOutput, calls=%fused_computation.21.clone.1 | convolution fusion | flops 204488704 | bytes 4391436 | tf_op jit(solution)/shard_map/while/body/eval_jaxpr/dot_general | solution.py:58
  81.7 5.1 fusion.232
  89.8 6.2 %fusion.231 = f32[16,32768]{1,0:T(8,128)} fusion(f32[16,32768]{1,0:T(8,128)} %get-tuple-element.1416, s32[]{:T(128)S(6)} %select_n.80, f32[4,1024,1024]{2,1,0:T(8,128)} %get-tuple-element.1428, s32[]{:T(128)S(6)} %copy.29, pred[]{:T(512)} %bitcast.292, f32[16,32768]{1,0:T(8,128)S(1)} %get-tuple-element.1427, s32[]{:T(128)S(6)} %select_n.81), kind=kOutput, calls=%fused_computation.21.clone.1 | convolution fusion | flops 204488704 | bytes 4391436 | tf_op jit(solution)/shard_map/while/body/eval_jaxpr/dot_general | solution.py:58
  96.0 5.1 fusion.232
  104.1 6.2 %fusion.231 = f32[16,32768]{1,0:T(8,128)} fusion(f32[16,32768]{1,0:T(8,128)} %get-tuple-element.1416, s32[]{:T(128)S(6)} %select_n.80, f32[4,1024,1024]{2,1,0:T(8,128)} %get-tuple-element.1428, s32[]{:T(128)S(6)} %copy.29, pred[]{:T(512)} %bitcast.292, f32[16,32768]{1,0:T(8,128)S(1)} %get-tuple-element.1427, s32[]{:T(128)S(6)} %select_n.81), kind=kOutput, calls=%fused_computation.21.clone.1 | convolution fusion | flops 204488704 | bytes 4391436 | tf_op jit(solution)/shard_map/while/body/eval_jaxpr/dot_general | solution.py:58
  110.3 5.1 fusion.232
  118.4 6.2 %fusion.231 = f32[16,32768]{1,0:T(8,128)} fusion(f32[16,32768]{1,0:T(8,128)} %get-tuple-element.1416, s32[]{:T(128)S(6)} %select_n.80, f32[4,1024,1024]{2,1,0:T(8,128)} %get-tuple-element.1428, s32[]{:T(128)S(6)} %copy.29, pred[]{:T(512)} %bitcast.292, f32[16,32768]{1,0:T(8,128)S(1)} %get-tuple-element.1427, s32[]{:T(128)S(6)} %select_n.81), kind=kOutput, calls=%fused_computation.21.clone.1 | convolution fusion | flops 204488704 | bytes 4391436 | tf_op jit(solution)/shard_map/while/body/eval_jaxpr/dot_general | solution.py:58
  124.7 5.1 fusion.232
  130.4 40.1 %all_gather.7 = f32[32768]{0:T(1024)S(1)} all-gather(f32[1024]{0:T(1024)S(1)} %copy-done.5), channel_id=1, replica_groups=mesh['grp'=4,'tile'=8] {'grp','tile'}, dimensions={0}, use_global_device_ids=true | all-gather | bytes 135168 | tf_op jit(solution)/shard_map/all_gather | solution.py:88
  174.8 88.8 %all-reduce.3.cloned.1.call-done = f32[16,32768]{1,0:T(8,128)} async-done(((f32[16,32768]{1,0:T(8,128)}), f32[16,32768]{1,0:T(8,128)}) %all-reduce.3.cloned.1.call-update) | async-done | bytes 2097168 | tf_op jit(solution)/shard_map/psum | solution.py:96
  263.6 4.5 fusion.55
  331.0 57.8 %while.116 = (s32[]{:T(128)}, f32[16,32768]{1,0:T(8,128)}, s32[4,2]{0,1:T(2,128)S(1)}, f32[16,32768]{1,0:T(8,128)}, f32[4,1024,1024]{2,1,0:T(8,128)}, /*index=5*/s32[]{:T(128)}, s32[1,1]{0,1:T(1,128)}, s32[]{:T(128)}, s32[]{:T(128)}) while((s32[]{:T(128)}, f32[16,32768]{1,0:T(8,128)}, s32[4,2]{0,1:T(2,128)S(1)}, ...), condition=%wide.region_4.5_spmd.clone, body=%wide.region_3.4_spmd.clone.sunk | while | flops 408977408 | bytes 8783110 | solution.py:80
  334.2 6.2 %fusion.236 = f32[16,32768]{1,0:T(8,128)} fusion(f32[16,32768]{1,0:T(8,128)} %get-tuple-element.1443, s32[]{:T(128)S(6)} %select_n.84, f32[4,1024,1024]{2,1,0:T(8,128)} %get-tuple-element.1455, s32[]{:T(128)S(6)} %copy.98, pred[]{:T(512)} %bitcast.297, f32[16,32768]{1,0:T(8,128)} %get-tuple-element.1454, s32[]{:T(128)S(6)} %select_n.85), kind=kOutput, calls=%fused_computation.46.clone.1 | convolution fusion | flops 204488704 | bytes 4391436 | tf_op jit(solution)/shard_map/while/body/eval_jaxpr/dot_general | solution.py:58
  340.4 5.1 fusion.237
  348.6 6.2 %fusion.236 = f32[16,32768]{1,0:T(8,128)} fusion(f32[16,32768]{1,0:T(8,128)} %get-tuple-element.1443, s32[]{:T(128)S(6)} %select_n.84, f32[4,1024,1024]{2,1,0:T(8,128)} %get-tuple-element.1455, s32[]{:T(128)S(6)} %copy.98, pred[]{:T(512)} %bitcast.297, f32[16,32768]{1,0:T(8,128)} %get-tuple-element.1454, s32[]{:T(128)S(6)} %select_n.85), kind=kOutput, calls=%fused_computation.46.clone.1 | convolution fusion | flops 204488704 | bytes 4391436 | tf_op jit(solution)/shard_map/while/body/eval_jaxpr/dot_general | solution.py:58
  354.9 5.1 fusion.237
  363.1 6.2 %fusion.236 = f32[16,32768]{1,0:T(8,128)} fusion(f32[16,32768]{1,0:T(8,128)} %get-tuple-element.1443, s32[]{:T(128)S(6)} %select_n.84, f32[4,1024,1024]{2,1,0:T(8,128)} %get-tuple-element.1455, s32[]{:T(128)S(6)} %copy.98, pred[]{:T(512)} %bitcast.297, f32[16,32768]{1,0:T(8,128)} %get-tuple-element.1454, s32[]{:T(128)S(6)} %select_n.85), kind=kOutput, calls=%fused_computation.46.clone.1 | convolution fusion | flops 204488704 | bytes 4391436 | tf_op jit(solution)/shard_map/while/body/eval_jaxpr/dot_general | solution.py:58
  369.3 5.1 fusion.237
  377.5 6.2 %fusion.236 = f32[16,32768]{1,0:T(8,128)} fusion(f32[16,32768]{1,0:T(8,128)} %get-tuple-element.1443, s32[]{:T(128)S(6)} %select_n.84, f32[4,1024,1024]{2,1,0:T(8,128)} %get-tuple-element.1455, s32[]{:T(128)S(6)} %copy.98, pred[]{:T(512)} %bitcast.297, f32[16,32768]{1,0:T(8,128)} %get-tuple-element.1454, s32[]{:T(128)S(6)} %select_n.85), kind=kOutput, calls=%fused_computation.46.clone.1 | convolution fusion | flops 204488704 | bytes 4391436 | tf_op jit(solution)/shard_map/while/body/eval_jaxpr/dot_general | solution.py:58
  383.7 5.1 fusion.237
  392.1 130.4 %all-reduce.5.cloned.1.call-done = f32[16,32768]{1,0:T(8,128)} async-done(((f32[16,32768]{1,0:T(8,128)}), f32[16,32768]{1,0:T(8,128)}) %all-reduce.5.cloned.1.call-update) | async-done | bytes 2097168 | tf_op jit(solution)/shard_map/psum | solution.py:96
  522.5 5.8 %fusion.54 = f32[16,16]{1,0:T(8,128)S(1)} fusion(f32[16,32768]{1,0:T(8,128)} %get-tuple-element.1465, f32[16,32768]{1,0:T(8,128)} %all-reduce.5.cloned.1.call-done, f32[32768]{0:T(1024)S(1)} %all_gather.7), kind=kOutput, calls=%fused_computation.60 | convolution fusion | flops 101711872 | bytes 4326400 | tf_op jit(solution)/shard_map/dot_general | solution.py:24
  (463 shorter events, 78.4 us)
Async XLA Ops:
  7.2 64.3 %copy-start.4 = (s32[4,2]{0,1:T(2,128)S(1)}, s32[4,2]{0,1:T(2,128)}, u32[]{:S(2)}) copy-start(s32[4,2]{0,1:T(2,128)} %param.197) | copy-start | bytes 100
  7.2 62.9 %all-gather.2.cloned.1.call-start = ((), (), s32[]{:S(2)}) async-start(), calls=%async_computation | async-start | bytes 2162688 | tf_op jit(solution)/shard_map/all_gather | solution.py:87
  7.9 255.7 %all-reduce.3.cloned.1.call-start = ((), (), s32[]{:S(2)}) async-start(), calls=%async_computation.1 | async-start | bytes 4194304 | tf_op jit(solution)/shard_map/psum | solution.py:96
  70.1 2.3 copy-start
  129.7 0.7 copy-start.5
  129.8 392.8 %all-reduce.5.cloned.1.call-start = ((), (), s32[]{:S(2)}) async-start(), calls=%async_computation.2 | async-start | bytes 4194304 | tf_op jit(solution)/shard_map/psum | solution.py:96
  299.2 2.8 copy-start.2
  522.5 32.3 %copy-start.1 = (f32[16,32768]{1,0:T(8,128)S(1)}, f32[16,32768]{1,0:T(8,128)}, u32[]{:S(2)}) copy-start(f32[16,32768]{1,0:T(8,128)} %get-tuple-element.1465) | copy-start | bytes 6291460
  554.8 1.9 copy-start.3
Sparse Core Ops, SparseCore 0:
  10.9 59.1 all-gather.1
  129.9 133.6 all-reduce.2
  389.0 133.5 all-reduce.4
where the time goes:
time: 569 us; the launch traced here: 568 us
  waiting for transfers between devices  282 us (50%)
  matrix products  122 us (21%)
  between operations  47.7 us (8%)
  local copies, waits for them, and re-layouts  40.6 us (7%)
  blocking collectives  40.1 us (7%)
  loops' own time  19.8 us (3%)
  other arithmetic  16.3 us (3%)
    psum x2, waiting for transfers between devices, local(): lax.psum(partial_image, ('grp', 'tile')) + whole_ridge[None, :] * direction  219 us
    all_gather x1, waiting for transfers between devices, local(): lax.all_gather(right_side, ('grp', 'tile'), axis=1, tiled=True)  62.1 us
    dot_general x8, matrix products, step(): lax.dot_general(from_col, direct_tile, (((1,), (1,)), ((), ())), precisio...  49.9 us
    dot_general x8, matrix products, step(): jnp.dot(from_row, mirror_tile, precision=lax.Precision.HIGHEST, preferred...  40.6 us
    all_gather x1, blocking collectives, local(): lax.all_gather(ridge, ('grp', 'tile'), axis=0, tiled=True)  40.1 us
    slice x48, local copies, waits for them, and re-layouts, gauss_solve(): scale = 1.0 / matrix[pivot, pivot]  28.1 us
    another operation x2, loops' own time, apply_kernel(): total, _ = lax.scan(step, start, (tiles, tile_list))  19.8 us
    dot_general x4, matrix products, gram(): lax.dot_general(left, right, (((1,), (1,)), ((), ())), precision=lax.Prec...  16.1 us
  transfers between devices with their start and end apart: 3, of which 3 were waited for; matrix products, arithmetic and copies ran while one was open for 1% of the time, Pallas kernels for 0%

commit v1 on v0

--- a/solution.py
+++ b/solution.py
@@ -93,7 +93,7 @@
     norm_now = gram(residual, residual)
     for step in range(ITERS):
         partial_image = apply_kernel(tiles, tile_list, direction)
-        image = lax.psum(partial_image, ("grp", "tile")) + whole_ridge[None, :] * direction
+        image = lax.psum(lax.psum(partial_image, "tile"), "grp") + whole_ridge[None, :] * direction
         alpha = gauss_solve(gram(direction, image), norm_now)
         solution = solution + mixed(alpha, direction)
         residual = residual - mixed(alpha, image)

time: 569 us -> 600 us (1.054)
  waiting for transfers between devices: 282 us -> 311 us
    psum x2 -> x4, waiting for transfers between devices: 219 us -> 248 us  [the longest x2 126 us: local(): lax.psum(lax.psum(partial_image, 'tile'), 'grp')]
  transfers between devices with their start and end apart: 3 -> 5, of which waited for: 3 -> 5; matrix products, arithmetic and copies ran while one was open for 1% -> 1% of each run, Pallas kernels for 0% -> 0%
where the time goes in v1:
time: 600 us; the launch traced here: 599 us
  waiting for transfers between devices  311 us (52%)
  matrix products  122 us (20%)
  between operations  47.8 us (8%)
  blocking collectives  42 us (7%)
  local copies, waits for them, and re-layouts  40 us (7%)
  loops' own time  20.4 us (3%)
  other arithmetic  16.3 us (3%)
    psum x2, waiting for transfers between devices, local(): lax.psum(lax.psum(partial_image, 'tile'), 'grp')  126 us
    psum x2, waiting for transfers between devices, local(): lax.psum(partial_image, 'tile')  122 us
    all_gather x1, waiting for transfers between devices, local(): lax.all_gather(right_side, ('grp', 'tile'), axis=1, tiled=True)  62.1 us
    dot_general x8, matrix products, step(): lax.dot_general(from_col, direct_tile, (((1,), (1,)), ((), ())), precisio...  49.9 us
    all_gather x1, blocking collectives, local(): lax.all_gather(ridge, ('grp', 'tile'), axis=0, tiled=True)  42 us
    dot_general x8, matrix products, step(): jnp.dot(from_row, mirror_tile, precision=lax.Precision.HIGHEST, preferred...  40.6 us
    slice x48, local copies, waits for them, and re-layouts, gauss_solve(): scale = 1.0 / matrix[pivot, pivot]  28.1 us
    another operation x2, loops' own time, apply_kernel(): total, _ = lax.scan(step, start, (tiles, tile_list))  20.4 us
  transfers between devices with their start and end apart: 5, of which 5 were waited for; matrix products, arithmetic and copies ran while one was open for 1% of the time, Pallas kernels for 0%

profile of v1, /device:TPU:0, one launch (start us, length us, event | category | flops | bytes accessed | tf_op | source)
XLA Modules:
  0.0 598.9 jit_solution(11250268382562658993)
XLA Ops:
  8.0 62.1 %all-gather.2.cloned.1.call-done = f32[16,32768]{1,0:T(8,128)} async-done(((f32[16,1024]{1,0:T(8,128)}), f32[16,32768]{1,0:T(8,128)}) %all-gather.2.cloned.1.call-update) | async-done | bytes 2097168 | tf_op jit(solution)/shard_map/all_gather | solution.py:87
  72.4 57.8 %while.115 = (s32[]{:T(128)}, f32[16,32768]{1,0:T(8,128)}, s32[4,2]{0,1:T(2,128)S(1)}, f32[16,32768]{1,0:T(8,128)S(1)}, f32[4,1024,1024]{2,1,0:T(8,128)}, /*inde...) while((s32[]{:T(128)}, f32[16,32768]{1,0:T(8,128)}, s32[4,2]{0,1:T(2,128)S(1)}, ...), condition=%wide.region_1.2_spmd.clone, body=%wide.region_0.1_spmd.clone.sunk | while | flops 408977408 | bytes 8783110 | solution.py:80
  75.6 6.2 %fusion.231 = f32[16,32768]{1,0:T(8,128)} fusion(f32[16,32768]{1,0:T(8,128)} %get-tuple-element.1416, s32[]{:T(128)S(6)} %select_n.80, f32[4,1024,1024]{2,1,0:T(8,128)} %get-tuple-element.1428, s32[]{:T(128)S(6)} %copy.29, pred[]{:T(512)} %bitcast.292, f32[16,32768]{1,0:T(8,128)S(1)} %get-tuple-element.1427, s32[]{:T(128)S(6)} %select_n.81), kind=kOutput, calls=%fused_computation.21.clone.1 | convolution fusion | flops 204488704 | bytes 4391436 | tf_op jit(solution)/shard_map/while/body/eval_jaxpr/dot_general | solution.py:58
  81.8 5.1 fusion.232
  90.0 6.2 %fusion.231 = f32[16,32768]{1,0:T(8,128)} fusion(f32[16,32768]{1,0:T(8,128)} %get-tuple-element.1416, s32[]{:T(128)S(6)} %select_n.80, f32[4,1024,1024]{2,1,0:T(8,128)} %get-tuple-element.1428, s32[]{:T(128)S(6)} %copy.29, pred[]{:T(512)} %bitcast.292, f32[16,32768]{1,0:T(8,128)S(1)} %get-tuple-element.1427, s32[]{:T(128)S(6)} %select_n.81), kind=kOutput, calls=%fused_computation.21.clone.1 | convolution fusion | flops 204488704 | bytes 4391436 | tf_op jit(solution)/shard_map/while/body/eval_jaxpr/dot_general | solution.py:58
  96.2 5.1 fusion.232
  104.5 6.2 %fusion.231 = f32[16,32768]{1,0:T(8,128)} fusion(f32[16,32768]{1,0:T(8,128)} %get-tuple-element.1416, s32[]{:T(128)S(6)} %select_n.80, f32[4,1024,1024]{2,1,0:T(8,128)} %get-tuple-element.1428, s32[]{:T(128)S(6)} %copy.29, pred[]{:T(512)} %bitcast.292, f32[16,32768]{1,0:T(8,128)S(1)} %get-tuple-element.1427, s32[]{:T(128)S(6)} %select_n.81), kind=kOutput, calls=%fused_computation.21.clone.1 | convolution fusion | flops 204488704 | bytes 4391436 | tf_op jit(solution)/shard_map/while/body/eval_jaxpr/dot_general | solution.py:58
  110.7 5.1 fusion.232
  118.9 6.2 %fusion.231 = f32[16,32768]{1,0:T(8,128)} fusion(f32[16,32768]{1,0:T(8,128)} %get-tuple-element.1416, s32[]{:T(128)S(6)} %select_n.80, f32[4,1024,1024]{2,1,0:T(8,128)} %get-tuple-element.1428, s32[]{:T(128)S(6)} %copy.29, pred[]{:T(512)} %bitcast.292, f32[16,32768]{1,0:T(8,128)S(1)} %get-tuple-element.1427, s32[]{:T(128)S(6)} %select_n.81), kind=kOutput, calls=%fused_computation.21.clone.1 | convolution fusion | flops 204488704 | bytes 4391436 | tf_op jit(solution)/shard_map/while/body/eval_jaxpr/dot_general | solution.py:58
  125.1 5.1 fusion.232
  130.3 60.8 %all-reduce.5.cloned.1.call-done = f32[16,32768]{1,0:T(8,128)} async-done(((f32[16,32768]{1,0:T(8,128)}), f32[16,32768]{1,0:T(8,128)}) %all-reduce.5.cloned.1.call-update) | async-done | bytes 2097168 | tf_op jit(solution)/shard_map/psum | solution.py:96
  191.2 42.0 %all_gather.7 = f32[32768]{0:T(1024)S(1)} all-gather(f32[1024]{0:T(1024)S(1)} %copy-done.5), channel_id=1, replica_groups=mesh['grp'=4,'tile'=8] {'grp','tile'}, dimensions={0}, use_global_device_ids=true | all-gather | bytes 135168 | tf_op jit(solution)/shard_map/all_gather | solution.py:88
  237.4 41.9 %all-reduce.7.cloned.1.call-done = f32[16,32768]{1,0:T(8,128)} async-done(((f32[16,32768]{1,0:T(8,128)}), f32[16,32768]{1,0:T(8,128)}) %all-reduce.7.cloned.1.call-update) | async-done | bytes 2097168 | tf_op jit(solution)/shard_map/psum | solution.py:96
  346.8 58.0 %while.116 = (s32[]{:T(128)}, f32[16,32768]{1,0:T(8,128)}, s32[4,2]{0,1:T(2,128)S(1)}, f32[16,32768]{1,0:T(8,128)}, f32[4,1024,1024]{2,1,0:T(8,128)}, /*index=5*/s32[]{:T(128)}, s32[1,1]{0,1:T(1,128)}, s32[]{:T(128)}, s32[]{:T(128)}) while((s32[]{:T(128)}, f32[16,32768]{1,0:T(8,128)}, s32[4,2]{0,1:T(2,128)S(1)}, ...), condition=%wide.region_5.6_spmd.clone, body=%wide.region_4.5_spmd.clone.sunk | while | flops 408977408 | bytes 8783110 | solution.py:80
  350.0 6.2 %fusion.236 = f32[16,32768]{1,0:T(8,128)} fusion(f32[16,32768]{1,0:T(8,128)} %get-tuple-element.1443, s32[]{:T(128)S(6)} %select_n.84, f32[4,1024,1024]{2,1,0:T(8,128)} %get-tuple-element.1455, s32[]{:T(128)S(6)} %copy.99, pred[]{:T(512)} %bitcast.297, f32[16,32768]{1,0:T(8,128)} %get-tuple-element.1454, s32[]{:T(128)S(6)} %select_n.85), kind=kOutput, calls=%fused_computation.46.clone.1 | convolution fusion | flops 204488704 | bytes 4391436 | tf_op jit(solution)/shard_map/while/body/eval_jaxpr/dot_general | solution.py:58
  364.5 6.2 %fusion.236 = f32[16,32768]{1,0:T(8,128)} fusion(f32[16,32768]{1,0:T(8,128)} %get-tuple-element.1443, s32[]{:T(128)S(6)} %select_n.84, f32[4,1024,1024]{2,1,0:T(8,128)} %get-tuple-element.1455, s32[]{:T(128)S(6)} %copy.99, pred[]{:T(512)} %bitcast.297, f32[16,32768]{1,0:T(8,128)} %get-tuple-element.1454, s32[]{:T(128)S(6)} %select_n.85), kind=kOutput, calls=%fused_computation.46.clone.1 | convolution fusion | flops 204488704 | bytes 4391436 | tf_op jit(solution)/shard_map/while/body/eval_jaxpr/dot_general | solution.py:58
  370.7 5.1 fusion.237
  379.0 6.2 %fusion.236 = f32[16,32768]{1,0:T(8,128)} fusion(f32[16,32768]{1,0:T(8,128)} %get-tuple-element.1443, s32[]{:T(128)S(6)} %select_n.84, f32[4,1024,1024]{2,1,0:T(8,128)} %get-tuple-element.1455, s32[]{:T(128)S(6)} %copy.99, pred[]{:T(512)} %bitcast.297, f32[16,32768]{1,0:T(8,128)} %get-tuple-element.1454, s32[]{:T(128)S(6)} %select_n.85), kind=kOutput, calls=%fused_computation.46.clone.1 | convolution fusion | flops 204488704 | bytes 4391436 | tf_op jit(solution)/shard_map/while/body/eval_jaxpr/dot_general | solution.py:58
  385.2 5.1 fusion.237
  393.5 6.2 %fusion.236 = f32[16,32768]{1,0:T(8,128)} fusion(f32[16,32768]{1,0:T(8,128)} %get-tuple-element.1443, s32[]{:T(128)S(6)} %select_n.84, f32[4,1024,1024]{2,1,0:T(8,128)} %get-tuple-element.1455, s32[]{:T(128)S(6)} %copy.99, pred[]{:T(512)} %bitcast.297, f32[16,32768]{1,0:T(8,128)} %get-tuple-element.1454, s32[]{:T(128)S(6)} %select_n.85), kind=kOutput, calls=%fused_computation.46.clone.1 | convolution fusion | flops 204488704 | bytes 4391436 | tf_op jit(solution)/shard_map/while/body/eval_jaxpr/dot_general | solution.py:58
  399.7 5.1 fusion.237
  404.8 60.8 %all-reduce.9.cloned.1.call-done = f32[16,32768]{1,0:T(8,128)} async-done(((f32[16,32768]{1,0:T(8,128)}), f32[16,32768]{1,0:T(8,128)}) %all-reduce.9.cloned.1.call-update) | async-done | bytes 2097168 | tf_op jit(solution)/shard_map/psum | solution.py:96
  469.0 84.2 %all-reduce.11.cloned.1.call-done = f32[16,32768]{1,0:T(8,128)} async-done(((f32[16,32768]{1,0:T(8,128)}), f32[16,32768]{1,0:T(8,128)}) %all-reduce.11.cloned.1.call-update) | async-done | bytes 2097168 | tf_op jit(solution)/shard_map/psum | solution.py:96
  553.1 5.8 fusion.54
  (469 shorter events, 87.7 us)
Async XLA Ops:
  7.2 64.4 %copy-start.4 = (s32[4,2]{0,1:T(2,128)S(1)}, s32[4,2]{0,1:T(2,128)}, u32[]{:S(2)}) copy-start(s32[4,2]{0,1:T(2,128)} %param.197) | copy-start | bytes 100
  7.2 62.9 %all-gather.2.cloned.1.call-start = ((), (), s32[]{:S(2)}) async-start(), calls=%async_computation | async-start | bytes 2162688 | tf_op jit(solution)/shard_map/all_gather | solution.py:87
  7.9 183.2 %all-reduce.5.cloned.1.call-start = ((), (), s32[]{:S(2)}) async-start(), calls=%async_computation.1 | async-start | bytes 4194304 | tf_op jit(solution)/shard_map/psum | solution.py:96
  70.1 2.3 copy-start
  130.2 61.0 %copy-start.5 = (f32[1024]{0:T(1024)S(1)}, f32[1024]{0:T(1024)}, u32[]{:S(2)}) copy-start(f32[1024]{0:T(1024)} %param.195) | copy-start | bytes 12292
  130.2 149.1 %all-reduce.7.cloned.1.call-start = ((), (), s32[]{:S(2)}) async-start(), calls=%async_computation.2 | async-start | bytes 4194304 | tf_op jit(solution)/shard_map/psum | solution.py:96
  191.1 274.6 %all-reduce.9.cloned.1.call-start = ((), (), s32[]{:S(2)}) async-start(), calls=%async_computation.3 | async-start | bytes 4194304 | tf_op jit(solution)/shard_map/psum | solution.py:96
  314.8 2.9 copy-start.2
  404.8 148.3 %all-reduce.11.cloned.1.call-start = ((), (), s32[]{:S(2)}) async-start(), calls=%async_computation.4 | async-start | bytes 4194304 | tf_op jit(solution)/shard_map/psum | solution.py:96
  553.1 32.3 %copy-start.1 = (f32[16,32768]{1,0:T(8,128)S(1)}, f32[16,32768]{1,0:T(8,128)}, u32[]{:S(2)}) copy-start(f32[16,32768]{1,0:T(8,128)} %get-tuple-element.1467) | copy-start | bytes 6291460
  585.4 1.9 copy-start.3
Sparse Core Ops, SparseCore 0:
  10.9 59.1 all-gather.1
  130.4 60.6 all-reduce.4
  193.5 85.7 all-reduce.6
  404.9 60.7 all-reduce.8
  467.9 85.1 all-reduce.10
